TPU v7x, 128 devices: a whole 4x4x4 slice. The times are simulated.
128 devices in a mesh: seq: 8 (over z, core), exp: 16 (over y, x).
Axes of the slice: x: 4, y: 4, z: 4, core: 2. Of those that a mesh axis runs over, the one named last changes fastest.
Arguments:
- inputs: bfloat16 [16, 1024, 4096], P('exp', 'seq'), may hold values from -6 to 6
- b_proj: bfloat16 [16, 1024, 128], P('exp', 'seq'), may hold values from -0.046875 to 0.046875
- c_proj: bfloat16 [16, 1024, 128], P('exp', 'seq'), may hold values from -6 to 6
- log_decay: float32 [16, 32, 1024], P('exp', None, 'seq'), may hold values from -1.1 to 0, as said below
- doc_lengths: int32 [16, 6], P('exp'), may hold values from 1 to 512, 1024 in all within a row
- expert_ids: int32 [16, 1024, 2], P('exp', 'seq'), may hold values from 0 to 15, all different within a row; in each aligned block of 128 rows (0 to 127, 128 to 255, ..., all dimensions but the last counted through in order) at most 24 rows name the same one
- gate_weights: float32 [16, 1024, 2], P('exp', 'seq'), may hold values from 0.2 to 1
- w_up: bfloat16 [16, 4096, 1024], P('exp'), may hold values from -0.09375 to 0.09375
- w_down: bfloat16 [16, 1024, 4096], P('exp'), may hold values from -0.1875 to 0.1875
- cotangent: bfloat16 [16, 1024, 4096], P('exp', 'seq'), may hold values from -6 to 6
Outputs:
- output: bfloat16 [16, 1024, 4096], P('exp', 'seq')
- input_grad: bfloat16 [16, 1024, 4096], P('exp', 'seq')
Inputs may be any that keep to these rules, and one draw needn't show every extreme that they name: `log_decay`: log of a decay factor, below zero. `doc_lengths`: each sequence's document lengths sum to 1024. `expert_ids`: two different experts a position; among the 128 positions of one device no expert is named more than 24 times, a bound that some block reaches.
All inputs are finite; a program needn't handle non-finite values.
Results may differ from a plain program's by a relative error of at most 0.013.
Values may be sent and summed in bfloat16 or wider, within the bound.
A program may use at most 128 MiB of HBM per device.

v0:
```python
import jax
import jax.numpy as jnp
from jax import lax
from jax.sharding import PartitionSpec as P

BLOCK = 128


EPSILON = 1e-06
HIGHEST_PREC = lax.Precision.HIGHEST


def carried_in(x, axis, combine, identity, reverse):
    length, index = (lax.axis_size(axis), lax.axis_index(axis))
    everything = jax.tree.map(
        lambda part, kind: lax.all_gather(part.astype(kind), axis),
        x,
        jax.tree.map(lambda a: jnp.bfloat16 if a.dtype == jnp.float32 else a.dtype, x),
    )
    start = jax.tree.map(
        lambda part, zero: jnp.broadcast_to(jnp.asarray(zero, part.dtype), part.shape), x, identity
    )

    def hop(k, before):
        at = length - 1 - k if reverse else k
        reached = at > index if reverse else at < index
        new = combine(
            before, jax.tree.map(lambda part, own: part[at].astype(own.dtype), everything, x)
        )
        return jax.tree.map(lambda a, b: jnp.where(reached, a, b), new, before)

    return lax.fori_loop(0, length, hop, start)


def combine(earlier, later):
    return (earlier[0] * later[0], later[0][:, None, None] * earlier[1] + later[1])


def doc_index(starts, element_offsets):
    return jnp.sum((starts[None, :] <= element_offsets[:, None]).astype(jnp.int32), axis=1) - 1


def block_terms(x_blocks, b_blocks, c_blocks, log_blocks, doc_of, doc_before):
    span_len = log_blocks.shape[2]
    cumulative = jnp.cumsum(log_blocks, axis=2)
    lower = jnp.arange(span_len)[:, None] >= jnp.arange(span_len)[None, :]
    same_doc = (doc_of[:, :, None] == doc_of[:, None, :]) & lower[None]
    spread = cumulative[:, :, :, None] - cumulative[:, :, None, :]
    decay_pairs = jnp.where(same_doc[:, None], jnp.exp(jnp.minimum(spread, 0.0)), 0.0)
    scores = jnp.einsum("ktn,ksn->kts", c_blocks, b_blocks, preferred_element_type=jnp.float32)
    mixing = (decay_pairs * scores[:, None]).astype(jnp.bfloat16)
    opened = (doc_of == doc_before[:, None]).astype(jnp.float32)
    tail_mask = (doc_of == doc_of[:, -1:]).astype(jnp.float32)
    last_cum = cumulative[:, :, -1:]
    c_weighted = (
        opened[:, None, :, None]
        * jnp.exp(cumulative)[..., None]
        * c_blocks[:, None].astype(jnp.float32)
    ).astype(jnp.bfloat16)
    b_weighted = (
        tail_mask[:, None, :, None]
        * jnp.exp(last_cum - cumulative)[..., None]
        * b_blocks[:, None].astype(jnp.float32)
    ).astype(jnp.bfloat16)
    retained = opened[:, -1:] * jnp.exp(last_cum[:, :, 0])
    local_state = jnp.einsum(
        "kshp,khsn->khpn", x_blocks, b_weighted, preferred_element_type=jnp.float32
    )
    return (mixing, c_weighted, b_weighted, retained, local_state)


def local_prefix(decays, states, backward):
    initial = (jnp.ones(decays.shape[1:], jnp.float32), jnp.zeros(states.shape[1:], jnp.float32))

    def advance(accumulated, element):
        return (combine(accumulated, element), accumulated)

    return lax.scan(advance, initial, (decays, states), reverse=backward)


def pass_states(overall, backward):
    identity = (jnp.ones_like(overall[0]), jnp.zeros_like(overall[1]))
    return carried_in(overall, "seq", combine, identity, backward)


def expert_forward(rows_in, expert_up, expert_down):
    pre_act = jnp.dot(rows_in, expert_up, preferred_element_type=jnp.float32)
    gate_sig = jax.nn.sigmoid(pre_act)
    activated = (pre_act * gate_sig).astype(jnp.bfloat16)
    expert_out = jnp.dot(activated, expert_down, preferred_element_type=jnp.float32).astype(
        jnp.bfloat16
    )
    return (expert_out, pre_act, gate_sig)


def expert_backward(pre_act, gate_sig, rows_grad, expert_up, expert_down):
    back_hidden = lax.dot_general(
        rows_grad, expert_down, (((1,), (1,)), ((), ())), preferred_element_type=jnp.float32
    )
    pre_grad = (back_hidden * gate_sig * (1.0 + pre_act * (1.0 - gate_sig))).astype(jnp.bfloat16)
    return lax.dot_general(
        pre_grad, expert_up, (((1,), (1,)), ((), ())), preferred_element_type=jnp.float32
    ).astype(jnp.bfloat16)


def expert_rows(rows_in, rows_grad, expert_up, expert_down):
    expert_out, pre_act, gate_sig = expert_forward(rows_in, expert_up, expert_down)
    return (expert_out, expert_backward(pre_act, gate_sig, rows_grad, expert_up, expert_down))


def send_back(expert_out, expert_grad):
    return (
        lax.all_to_all(expert_out, "exp", split_axis=0, concat_axis=0, tiled=True),
        lax.all_to_all(expert_grad, "exp", split_axis=0, concat_axis=0, tiled=True),
    )


def on_device(
    inputs,
    b_proj,
    c_proj,
    log_decay,
    doc_lengths,
    expert_ids,
    gate_weights,
    w_up,
    w_down,
    cotangent,
):
    tokens_here = inputs.shape[1]
    feature_count = inputs.shape[2]
    head_count = log_decay.shape[1]
    head_size = feature_count // head_count
    state_size = b_proj.shape[2]
    block_count = tokens_here // BLOCK
    expert_count = lax.axis_size("exp")
    capacity = 3 * tokens_here // expert_count
    lengths_here = doc_lengths[0]
    starts = jnp.cumsum(lengths_here) - lengths_here
    first_pos = lax.axis_index("seq") * tokens_here
    doc_of = doc_index(starts, first_pos + jnp.arange(tokens_here, dtype=jnp.int32)).reshape(
        block_count, BLOCK
    )
    doc_before = doc_index(starts, first_pos + jnp.arange(block_count, dtype=jnp.int32) * BLOCK - 1)
    x_blocks = inputs[0].reshape(block_count, BLOCK, head_count, head_size)
    log_blocks = log_decay[0].reshape(head_count, block_count, BLOCK).transpose(1, 0, 2)
    mixing, c_weighted, b_weighted, retained, local_state = block_terms(
        x_blocks,
        b_proj[0].reshape(block_count, BLOCK, state_size),
        c_proj[0].reshape(block_count, BLOCK, state_size),
        log_blocks,
        doc_of,
        doc_before,
    )
    overall, before = local_prefix(retained, local_state, False)
    arriving = pass_states(overall, False)
    state_in = before[0][:, :, None, None] * arriving[1][None] + before[1]
    inner = jnp.einsum("khts,kshp->kthp", mixing, x_blocks, preferred_element_type=jnp.float32)
    carried = jnp.einsum(
        "khpn,khtn->kthp", state_in, c_weighted.astype(jnp.float32), precision=HIGHEST_PREC
    )
    resid = (inner + carried).astype(jnp.bfloat16).reshape(tokens_here, feature_count)
    resid_rows = resid.astype(jnp.float32)
    scale_rows = lax.rsqrt(jnp.mean(resid_rows * resid_rows, axis=1, keepdims=True) + EPSILON)
    normed = resid_rows * scale_rows
    mixed_in = normed.astype(jnp.bfloat16)
    expert_flat = expert_ids[0].reshape(-1)
    one_hot = (expert_flat[:, None] == jnp.arange(expert_count, dtype=jnp.int32)[None, :]).astype(
        jnp.int32
    )
    slot_rank = jnp.sum((jnp.cumsum(one_hot, axis=0) - one_hot) * one_hot, axis=1)
    slot_of = expert_flat * capacity + slot_rank
    slot_owner = (
        jnp.full((expert_count * capacity,), tokens_here, jnp.int32)
        .at[slot_of]
        .set(jnp.arange(2 * tokens_here, dtype=jnp.int32) // 2)
    )
    pad_rows = jnp.zeros((1, feature_count), jnp.bfloat16)
    sent_in = jnp.concatenate([mixed_in, pad_rows])[slot_owner].reshape(
        expert_count, capacity, feature_count
    )
    sent_grad = jnp.concatenate([cotangent[0], pad_rows])[slot_owner].reshape(
        expert_count, capacity, feature_count
    )
    expert_up = w_up[0]
    expert_down = w_down[0]
    total_rows = expert_count * capacity
    got_in = lax.all_to_all(sent_in, "exp", split_axis=0, concat_axis=0, tiled=True)
    got_grad = lax.all_to_all(sent_grad, "exp", split_axis=0, concat_axis=0, tiled=True)
    slot_count = got_in.shape[1]
    expert_out, expert_grad = expert_rows(
        got_in.reshape(-1, feature_count),
        got_grad.reshape(-1, feature_count),
        expert_up,
        expert_down,
    )
    back_out, back_grad = send_back(
        expert_out.reshape(expert_count, slot_count, feature_count),
        expert_grad.reshape(expert_count, slot_count, feature_count),
    )
    got_out = back_out.reshape(total_rows, feature_count)[slot_of].reshape(
        tokens_here, 2, feature_count
    )
    got_back = back_grad.reshape(total_rows, feature_count)[slot_of].reshape(
        tokens_here, 2, feature_count
    )
    pair_weights = gate_weights[0][:, :, None]
    moe_rows = jnp.sum(pair_weights * got_out.astype(jnp.float32), axis=1)
    dmixed = jnp.sum(pair_weights * got_back.astype(jnp.float32), axis=1)
    output = (resid_rows + moe_rows).astype(jnp.bfloat16)
    dresid = (
        cotangent[0].astype(jnp.float32)
        + scale_rows * (dmixed - normed * jnp.mean(dmixed * normed, axis=1, keepdims=True))
    ).astype(jnp.bfloat16)
    grad_blocks = dresid.reshape(block_count, BLOCK, head_count, head_size)
    sources = jnp.einsum(
        "kthp,khtn->khpn", grad_blocks, c_weighted, preferred_element_type=jnp.float32
    )
    overall_back, after_local = local_prefix(retained, sources, True)
    arriving_back = pass_states(overall_back, True)
    state_after = after_local[0][:, :, None, None] * arriving_back[1][None] + after_local[1]
    inner_back = jnp.einsum(
        "khts,kthp->kshp", mixing, grad_blocks, preferred_element_type=jnp.float32
    )
    carried_back = jnp.einsum(
        "khpn,khsn->kshp", state_after, b_weighted.astype(jnp.float32), precision=HIGHEST_PREC
    )
    input_grad = (
        (inner_back + carried_back).astype(jnp.bfloat16).reshape(tokens_here, feature_count)
    )
    return (output[None], input_grad[None])


def solution(mesh):
    placed = (
        P("exp", "seq", None),
        P("exp", "seq", None),
        P("exp", "seq", None),
        P("exp", None, "seq"),
        P("exp", None),
        P("exp", "seq", None),
        P("exp", "seq", None),
        P("exp", None, None),
        P("exp", None, None),
        P("exp", "seq", None),
    )
    return jax.shard_map(
        on_device,
        mesh=mesh,
        in_specs=placed,
        out_specs=(P("exp", "seq", None), P("exp", "seq", None)),
        check_vma=False,
    )
```

profile of v0, /device:TPU:1, one launch (start us, length us, event | category | flops | bytes accessed | tf_op | source)
XLA Modules:
  0.0 431.8 jit_solution(498204873898748437)
XLA Ops:
  20.0 13.2 %all-gather = bf16[8,32,1]{1,2,0:T(2,128)(2,1)S(1)} all-gather(bf16[1,32,1]{1,2,0:T(2,128)(2,1)S(1)} %multiply_convert_fusion.15), channel_id=2, replica_groups=mesh['seq'=8,'exp'=16] {'seq'}, dimensions={0}, use_global_device_ids=true | all-gather | bytes 576 | tf_op jit(solution)/shard_map/all_gather | solution.py:16
  36.0 2.9 fusion.32
  38.9 34.3 %all-gather.6.cloned.1.call-done = bf16[256,128,128]{2,1,0:T(8,128)(2,1)} async-done(((bf16[32,128,128]{2,1,0:T(8,128)(2,1)}), bf16[256,128,128]{2,1,0:T(8,128)(2,1)}) %all-gather.6.cloned.1.call-update) | async-done | bytes 8388624 | tf_op jit(solution)/shard_map/all_gather | solution.py:16
  73.2 18.0 %while.20 = (s32[]{:T(128)}, f32[32,128,128]{2,1,0:T(8,128)S(1)}, s32[]{:T(128)}, bf16[8,32]{1,0:T(8,128)(2,1)S(1)}, bf16[8,32,128,128]{3,2,1,0:T(8,128)(2,1)}, /*index=5*/s32[]{:T(128)}, s32[]{:T(128)}) while((s32[]{:T(128)}, f32[32,128,128]{2,1,0:T(8,128)S(1)}, s32[]{:T(128)}, bf16[8,32]{1,0:T(8,128)(2,1)S(1)}, ...), condition=%wide.region_5.6_spmd.clone, body=%wide.region_4.5_spmd.clone.sunk | while | flops 2621476 | bytes 5243313 | solution.py:32
  77.7 2.2 fusion.63
  80.0 2.2 fusion.63
  82.2 2.2 fusion.63
  91.2 4.8 %fusion.54 = (f32[1,128,32,128]{1,3,2,0:T(8,128)}, bf16[1,128,32,128]{1,3,2,0:T(8,128)(2,1)S(1)}) fusion(f32[32,128,128]{2,1,0:T(8,128)S(1)} %get-tuple-element.270, f32[128,128]{1,0:T(8,128)S(1)} %bitcast_convert_fusion.3, f32[32,128]{1,0:T(8,128)S(1)} %get-tuple-element.350, f32[32,128,128]{1,2,0:T(8,128)} %fusion.32), kind=kOutput, calls=%fused_computation.104 | convolution fusion | flops 807927808 | bytes 7421952 | tf_op jit(solution)/shard_map/khpn,khtn->kthp/dot_general | solution.py:159
  96.0 2.3 copy.70
  99.3 4.1 gather_fusion
  103.4 6.7 %all-to-all-start = ((bf16[16,24,4096]{2,1,0:T(8,128)(2,1)}), bf16[16,24,4096]{2,1,0:T(8,128)(2,1)}, u32[]{:S(2)}, u32[]{:S(2)}) async-start(bf16[16,24,4096]{2,1,0:T(8,128)(2,1)} %bitcast.144), calls=%async_computation | async-start | bytes 6291456 | tf_op jit(solution)/shard_map/all_to_all | solution.py:188
  110.2 4.1 gather_fusion.2
  114.3 43.7 %all-to-all-done = bf16[16,24,4096]{2,1,0:T(8,128)(2,1)} async-done(((bf16[16,24,4096]{2,1,0:T(8,128)(2,1)}), bf16[16,24,4096]{2,1,0:T(8,128)(2,1)}, u32[]{:S(2)}, u32[]{:S(2)}) %all-to-all-start) | async-done | bytes 3145760 | tf_op jit(solution)/shard_map/all_to_all | solution.py:188
  158.0 4.1 all-to-all-start.2
  162.1 8.9 %fusion.8 = f32[384,1024]{1,0:T(8,128)} fusion(bf16[384,4096]{1,0:T(8,128)(2,1)} %bitcast.22, bf16[1,4096,1024]{2,1,0:T(8,128)(2,1)} %param.21), kind=kOutput, calls=%fused_computation.17 | convolution fusion | flops 3221225472 | bytes 13107200 | tf_op jit(solution)/shard_map/dot_general | solution.py:87
  171.0 36.0 %all-to-all-done.2 = bf16[16,24,4096]{2,1,0:T(8,128)(2,1)S(1)} async-done(((bf16[16,24,4096]{2,1,0:T(8,128)(2,1)}), bf16[16,24,4096]{2,1,0:T(8,128)(2,1)S(1)}, u32[]{:S(2)}, u32[]{:S(2)}) %all-to-all-start.2) | async-done | bytes 3145760 | tf_op jit(solution)/shard_map/all_to_all | solution.py:189
  207.0 18.5 %fusion.10 = bf16[384,4096]{1,0:T(8,128)(2,1)} fusion(bf16[1,4096,1024]{2,1,0:T(8,128)(2,1)} %param.21, f32[384,1024]{1,0:T(8,128)} %fusion.8, bf16[384,4096]{1,0:T(8,128)(2,1)S(1)} %bitcast.151, bf16[1,1024,4096]{2,1,0:T(8,128)(2,1)} %param.22), kind=kOutput, calls=%fused_computation.19 | convolution fusion | flops 6447562752 | bytes 24641536 | tf_op jit(solution)/shard_map/dot_general | solution.py:101
  225.5 3.7 all-to-all-start.3
  229.2 9.0 %fusion.13 = bf16[384,4096]{1,0:T(8,128)(2,1)} fusion(bf16[1,1024,4096]{2,1,0:T(8,128)(2,1)} %param.22, f32[384,1024]{1,0:T(8,128)} %fusion.8), kind=kOutput, calls=%fused_computation.20 | convolution fusion | flops 3224764416 | bytes 13107200 | tf_op jit(solution)/shard_map/dot_general | solution.py:90
  238.2 32.9 %all-to-all-done.3 = bf16[16,24,4096]{2,1,0:T(8,128)(2,1)S(1)} async-done(((bf16[16,24,4096]{2,1,0:T(8,128)(2,1)}), bf16[16,24,4096]{2,1,0:T(8,128)(2,1)S(1)}, u32[]{:S(2)}, u32[]{:S(2)}) %all-to-all-start.3) | async-done | bytes 3145760 | tf_op jit(solution)/shard_map/all_to_all | solution.py:114
  271.1 5.6 %all-to-all-start.1 = ((bf16[16,24,4096]{2,1,0:T(8,128)(2,1)}), bf16[16,24,4096]{2,1,0:T(8,128)(2,1)}, u32[]{:S(2)}, u32[]{:S(2)}) async-start(bf16[16,24,4096]{2,1,0:T(8,128)(2,1)} %bitcast.150), calls=%async_computation.1 | async-start | bytes 6291456 | tf_op jit(solution)/shard_map/all_to_all | solution.py:113
  277.0 2.6 copy.76
  279.7 3.2 gather_fusion.3
  282.9 5.4 %reshape.539 = f32[128,2,4096]{2,1,0:T(2,128)} reshape(bf16[256,4096]{1,0:T(8,128)(2,1)} %gather_fusion.3) | data formatting | bytes 6291456 | tf_op jit(solution)/shard_map/convert_element_type | solution.py:209
  288.3 30.5 %all-to-all-done.1 = bf16[16,24,4096]{2,1,0:T(8,128)(2,1)} async-done(((bf16[16,24,4096]{2,1,0:T(8,128)(2,1)}), bf16[16,24,4096]{2,1,0:T(8,128)(2,1)}, u32[]{:S(2)}, u32[]{:S(2)}) %all-to-all-start.1) | async-done | bytes 3145760 | tf_op jit(solution)/shard_map/all_to_all | solution.py:113
  318.8 6.2 %gather_fusion.1 = bf16[256,4096]{1,0:T(8,128)(2,1)S(1)} fusion(bf16[384,4096]{1,0:T(8,128)(2,1)} %bitcast.26, s32[1024]{0:T(1024)S(1)} %pad_clamp_fusion), kind=kCustom, calls=%fused_computation.1 | custom fusion | bytes 4195328 | tf_op jit(solution)/shard_map/gather | solution.py:201
  325.0 4.0 reshape.537
  329.0 15.2 %multiply_reduce_fusion = (f32[128,4096]{1,0:T(8,128)}, f32[128,4096]{1,0:T(8,128)}) fusion(f32[128,2,4096]{2,1,0:T(2,128)} %reshape.539, f32[128,2]{1,0:T(8,128)S(1)} %copy.69, f32[128,2,4096]{2,1,0:T(2,128)} %reshape.537), kind=kLoop, calls=%fused_computation.21 | loop fusion | flops 3145728 | bytes 12583936 | tf_op jit(solution)/shard_map/reduce_sum | solution.py:209
  351.4 3.2 copy.75
  358.7 43.0 %all-gather.8.cloned.1.call-done = bf16[256,128,128]{2,1,0:T(8,128)(2,1)} async-done(((bf16[32,128,128]{2,1,0:T(8,128)(2,1)}), bf16[256,128,128]{2,1,0:T(8,128)(2,1)}) %all-gather.8.cloned.1.call-update) | async-done | bytes 8388624 | tf_op jit(solution)/shard_map/all_gather | solution.py:16
  401.8 18.0 %while.21 = (s32[]{:T(128)}, f32[32,128,128]{2,1,0:T(8,128)S(1)}, s32[]{:T(128)}, bf16[8,32]{1,0:T(8,128)(2,1)S(1)}, bf16[8,32,128,128]{3,2,1,0:T(8,128)(2,1)}, ...) while((s32[]{:T(128)}, f32[32,128,128]{2,1,0:T(8,128)S(1)}, s32[]{:T(128)}, ...), condition=%wide.region_15.16_spmd.clone, body=%wide.region_14.15_spmd.clone.sunk | while | flops 2621480 | bytes 5243375 | solution.py:32
  419.8 3.8 fusion.16
  (114 shorter events, 57.0 us)
Async XLA Ops:
  7.2 66.0 %all-gather.6.cloned.1.call-start = ((), (), s32[]{:S(2)}) async-start(), calls=%async_computation.4 | async-start | bytes 9437184 | tf_op jit(solution)/shard_map/all_gather | solution.py:16
  18.2 1.4 copy-start.10
  18.2 17.7 %copy-start.9 = (bf16[1,128,128]{2,1,0:T(8,128)(2,1)S(1)}, bf16[1,128,128]{2,1,0:T(8,128)(2,1)}, u32[]{:S(2)}) copy-start(bf16[1,128,128]{2,1,0:T(8,128)(2,1)} %param.16) | copy-start | bytes 98308
  18.2 17.7 %copy-start.8 = (bf16[1,128,128]{2,1,0:T(8,128)(2,1)S(1)}, bf16[1,128,128]{2,1,0:T(8,128)(2,1)}, u32[]{:S(2)}) copy-start(bf16[1,128,128]{2,1,0:T(8,128)(2,1)} %param.15) | copy-start | bytes 98308
  96.0 2.3 copy-start
  103.4 6.7 %copy-start.5 = (bf16[1,128,4096]{2,1,0:T(8,128)(2,1)S(1)}, bf16[1,128,4096]{2,1,0:T(8,128)(2,1)}, u32[]{:S(2)}) copy-start(bf16[1,128,4096]{2,1,0:T(8,128)(2,1)} %param.23) | copy-start | bytes 3145732
  103.4 54.6 %all-to-all-start = ((bf16[16,24,4096]{2,1,0:T(8,128)(2,1)}), bf16[16,24,4096]{2,1,0:T(8,128)(2,1)}, u32[]{:S(2)}, u32[]{:S(2)}) async-start(bf16[16,24,4096]{2,1,0:T(8,128)(2,1)} %bitcast.144), calls=%async_computation | async-start | bytes 6291456 | tf_op jit(solution)/shard_map/all_to_all | solution.py:188
  158.0 49.0 %all-to-all-start.2 = ((bf16[16,24,4096]{2,1,0:T(8,128)(2,1)}), bf16[16,24,4096]{2,1,0:T(8,128)(2,1)S(1)}, u32[]{:S(2)}, u32[]{:S(2)}) async-start(bf16[16,24,4096]{2,1,0:T(8,128)(2,1)} %bitcast.143), calls=%async_computation.2 | async-start | bytes 6291456 | tf_op jit(solution)/shard_map/all_to_all | solution.py:189
  225.5 45.6 %all-to-all-start.3 = ((bf16[16,24,4096]{2,1,0:T(8,128)(2,1)}), bf16[16,24,4096]{2,1,0:T(8,128)(2,1)S(1)}, u32[]{:S(2)}, u32[]{:S(2)}) async-start(bf16[16,24,4096]{2,1,0:T(8,128)(2,1)} %bitcast.152), calls=%async_computation.3 | async-start | bytes 6291456 | tf_op jit(solution)/shard_map/all_to_all | solution.py:114
  271.1 47.7 %all-to-all-start.1 = ((bf16[16,24,4096]{2,1,0:T(8,128)(2,1)}), bf16[16,24,4096]{2,1,0:T(8,128)(2,1)}, u32[]{:S(2)}, u32[]{:S(2)}) async-start(bf16[16,24,4096]{2,1,0:T(8,128)(2,1)} %bitcast.150), calls=%async_computation.1 | async-start | bytes 6291456 | tf_op jit(solution)/shard_map/all_to_all | solution.py:113
  276.7 2.8 copy-start.11
  276.7 125.0 %all-gather.8.cloned.1.call-start = ((), (), s32[]{:S(2)}) async-start(), calls=%async_computation.5 | async-start | bytes 9437184 | tf_op jit(solution)/shard_map/all_gather | solution.py:16
  344.2 2.0 copy-start.1
  346.2 1.6 copy-start.2
  348.4 1.0 copy-start.6
  351.3 3.2 copy-start.7
  354.5 2.2 copy-start.3
  354.6 3.0 copy-start.4
Sparse Core Ops, SparseCore 0:
  19.7 53.4 all-gather.5
  351.5 50.2 all-gather.7
where the time goes:
time: 433 us; the launch traced here: 432 us
  waiting for transfers between devices  220 us (51%)
  other arithmetic  59.4 us (14%)
  matrix products  54.3 us (13%)
  local copies, waits for them, and re-layouts  47.7 us (11%)
  starting transfers between devices  20.5 us (5%)
  between operations  15.7 us (4%)
  blocking collectives  13.2 us (3%)
    all_gather x2, waiting for transfers between devices, carried_in(): lax.all_gather(part.astype(kind), axis)  77.3 us
    all_to_all x1, waiting for transfers between devices, on_device(): lax.all_to_all(sent_in, 'exp', split_axis=0, concat_axis=0, tiled=True)  43.7 us
    all_to_all x1, waiting for transfers between devices, on_device(): lax.all_to_all(sent_grad, 'exp', split_axis=0, concat_axis=0, tiled=True)  36 us
    select_n x16, other arithmetic, hop(): return jax.tree.map(lambda a, b: jnp.where(reached, a, b), new, before)  35.3 us
    all_to_all x1, waiting for transfers between devices, send_back(): lax.all_to_all(expert_grad, 'exp', split_axis=0, concat_axis=0, tiled=True)  32.9 us
    all_to_all x1, waiting for transfers between devices, send_back(): lax.all_to_all(expert_out, 'exp', split_axis=0, concat_axis=0, tiled=True)  30.5 us
    dot_general x1, matrix products, expert_backward(): lax.dot_general(pre_grad, expert_up, (((1,), (1,)), ((), ())), preferred_...  18.5 us
    reduce_sum x1, other arithmetic, on_device(): dmixed = jnp.sum(pair_weights * got_back.astype(jnp.float32), axis=1)  15.2 us
  transfers between devices with their start and end apart: 6, of which 6 were waited for; matrix products, arithmetic and copies ran while one was open for 11% of the time, Pallas kernels for 0%

commit v1 on v0

v1 whole, which is shorter than its diff:
```python
import functools
import jax
import jax.numpy as jnp
from jax import lax
from jax.experimental import pallas as pl
from jax.experimental.pallas import tpu as pltpu
from jax.sharding import PartitionSpec as P

MESH = pl.DeviceIdType.MESH
F32, BF16, I32 = jnp.float32, jnp.bfloat16, jnp.int32
HIGHEST = lax.Precision.HIGHEST
EPSILON = 1e-06

T = 128
D = 4096
HID = 1024
H = 32
CAP = 24
SLOTS = 16 * CAP
NSEQ = 8
CHUNKS = 8
CW = D // CHUNKS
HALF = D // 2
VMEM_LIMIT = 62 * 1024 * 1024

NEAR = [(dx, dy) for dx in (0, 1, 3) for dy in (0, 1, 3) if (dx, dy) != (0, 0)]
FAR = [(dx, dy) for dx in range(4) for dy in range(4) if 2 in (dx, dy)]
ORDER = [(0, 0)] + NEAR + FAR


def code_row(d):
    return (d[1] * 4 + d[0]) * CAP


def slot_row(d):
    return ORDER.index(d) * CAP


def flip(d):
    return ((4 - d[0]) % 4, (4 - d[1]) % 4)


def place():
    me = lax.axis_index("exp")
    return lax.axis_index("seq"), lax.rem(me, 4), me // 4


def at(here, d):
    seq, x, y = here
    return (seq, lax.rem(y + d[1], 4) * 4 + lax.rem(x + d[0], 4))


def entry_barrier(here, with_chain):
    barrier = pltpu.get_barrier_semaphore()
    for d in NEAR:
        pl.semaphore_signal(barrier, inc=1, device_id=at(here, d), device_id_type=MESH)
    count = len(NEAR)
    if with_chain:
        for k in (1, NSEQ - 1):
            peer = (lax.rem(here[0] + k, NSEQ), lax.axis_index("exp"))
            pl.semaphore_signal(barrier, inc=1, device_id=peer, device_id_type=MESH)
        count += 2
    pl.semaphore_wait(barrier, count)


EXCHANGE_SEMS = [
    pltpu.SemaphoreType.DMA((2, len(NEAR))),
    pltpu.SemaphoreType.DMA((2, len(FAR), 2)),
    pltpu.SemaphoreType.DMA((2, len(FAR), 2)),
    pltpu.SemaphoreType.DMA((1,)),
]


class Exchange:
    def __init__(self, here, src, dst, stage, sems, back):
        near_sem, far_sem, fwd_sem, self_sem = sems
        src_row, dst_row = (slot_row, code_row) if back else (code_row, slot_row)

        def rows(ref, start):
            return ref.at[pl.ds(start, CAP)]

        self.own = pltpu.make_async_copy(
            rows(src, src_row((0, 0))), rows(dst, dst_row((0, 0))), self_sem.at[0]
        )
        self.near = {}
        for k, d in enumerate(NEAR):
            self.near[d] = pltpu.make_async_remote_copy(
                rows(src, src_row(d)),
                rows(dst, dst_row(d)),
                near_sem.at[0, k],
                near_sem.at[1, k],
                device_id=at(here, flip(d) if back else d),
                device_id_type=MESH,
            )
        self.far, self.fwd = ([], [])
        for j, d in enumerate(FAR):
            v = flip(d) if back else d
            for q, sign in enumerate((1, 3)):
                leg = tuple(sign if a == 2 else a for a in v)
                rest = tuple((a - b) % 4 for a, b in zip(v, leg))
                cols = pl.ds(q * HALF, HALF)
                self.far.append(
                    pltpu.make_async_remote_copy(
                        src.at[pl.ds(src_row(d), CAP), cols],
                        stage.at[j, q],
                        far_sem.at[0, j, q],
                        far_sem.at[1, j, q],
                        device_id=at(here, leg),
                        device_id_type=MESH,
                    )
                )
                self.fwd.append(
                    pltpu.make_async_remote_copy(
                        stage.at[j, q],
                        dst.at[pl.ds(dst_row(d), CAP), cols],
                        fwd_sem.at[0, j, q],
                        fwd_sem.at[1, j, q],
                        device_id=at(here, rest),
                        device_id_type=MESH,
                    )
                )

    def start_far(self):
        for c in self.far:
            c.start()

    def start_near(self, which):
        for d in which:
            if d == (0, 0):
                self.own.start()
            else:
                self.near[d].start()

    def forward(self):
        for c, f in zip(self.far, self.fwd):
            c.wait_recv()
            f.start()

    def wait_near(self, which):
        for d in which:
            if d == (0, 0):
                self.own.wait()
            else:
                self.near[d].wait_recv()

    def wait_far(self):
        for f in self.fwd:
            f.wait_recv()

    def finish(self):
        for c in list(self.near.values()) + self.far + self.fwd:
            c.wait_send()


def iota(shape, dim):
    return lax.broadcasted_iota(I32, shape, dim)


def nt(a, b, precision=None):
    return lax.dot_general(
        a, b, (((1,), (1,)), ((), ())), precision=precision, preferred_element_type=F32
    )


def nn(a, b, precision=None):
    return jnp.dot(a, b, precision=precision, preferred_element_type=F32)


def slot_columns(ids_ref, here):
    seq, x, y = here
    codes = []
    for j in range(2):
        e = ids_ref[:, j : j + 1]
        codes.append((((e // 4) - y) & 3) * 4 + ((e & 3) - x & 3))
    lane = iota((T, T), 1)
    named = [lane == code for code in codes]
    both = jnp.where(named[0] | named[1], 1.0, 0.0).astype(BF16)
    earlier = jnp.where(iota((T, T), 1) < iota((T, T), 0), 1.0, 0.0).astype(BF16)
    rank = nn(earlier, both)
    return [
        code * CAP + jnp.sum(jnp.where(n, rank, 0.0), axis=1, keepdims=True).astype(I32)
        for code, n in zip(codes, named)
    ]


def pick_matrix(slots):
    eye = iota((T, T), 0) == iota((T, T), 1)
    s = iota((SLOTS, T), 0)
    hit = None
    for slot in slots:
        row = jnp.sum(jnp.where(eye, slot, 0), axis=0, keepdims=True)
        hit = (s == row) if hit is None else hit | (s == row)
    return jnp.where(hit, 1.0, 0.0).astype(BF16)


def weight_matrices(slots, gate_ref):
    s = iota((T, SLOTS), 1)
    w = jnp.zeros((T, SLOTS), F32)
    for j, slot in enumerate(slots):
        w = w + jnp.where(s == slot, gate_ref[:, j : j + 1], 0.0)
    high = w.astype(BF16)
    return high, (w - high.astype(F32)).astype(BF16)


def doc_facts(len_ref, seq):
    base = seq * T
    starts = [jnp.int32(0)]
    for j in range(5):
        starts.append(starts[-1] + len_ref[0, j])

    def doc(pos):
        total = jnp.where(starts[0] <= pos, 1, 0)
        for s in starts[1:]:
            total = total + jnp.where(s <= pos, 1, 0)
        return total - 1

    row, col = doc(base + iota((1, T), 1)), doc(base + iota((T, 1), 0))
    return row, col, doc(base - 1), doc(base + T - 1)


def local_terms(fwd, facts, ld_ref, b, c, rhs_ref, inner_ref, local_ref, col_ref, kept_ref):
    doc_row, doc_col, before, last_doc = facts
    down, across = iota((T, T), 0), iota((T, T), 1)
    own, other = (c, b) if fwd else (b, c)
    causal = (down >= across) if fwd else (across >= down)
    scores = jnp.where(causal & (doc_col == doc_row), nt(own, other), 0.0)
    eye = jnp.where(down == across, 1.0, 0.0).astype(BF16)
    turned = nt(eye, other)
    upto = jnp.where(down <= across, 1.0, 0.0)
    upto_t = jnp.where(across <= down, 1.0, 0.0)
    opened_e = jnp.where(last_doc == before, 1.0, 0.0)
    if fwd:
        row_mask = jnp.where(doc_row == last_doc, 1.0, 0.0)
        col_mask = jnp.where(doc_col == before, 1.0, 0.0)
    else:
        row_mask = jnp.where(doc_row == before, 1.0, 0.0)
        col_mask = jnp.where(doc_col == last_doc, 1.0, 0.0)

    def group(g, _):
        ld = ld_ref[pl.ds(pl.multiple_of(g * 8, 8), 8), :]
        crow = nn(ld, upto, HIGHEST)
        ccol = nt(upto_t, ld, HIGHEST)
        last = crow[:, T - 1 : T]
        if fwd:
            frow = row_mask * jnp.exp(last - crow)
            gcol = col_mask * jnp.exp(ccol)
        else:
            frow = row_mask * jnp.exp(crow)
            gcol = col_mask * jnp.exp(ccol[T - 1 : T, :] - ccol)
        col_ref[g] = gcol
        kept = opened_e * jnp.exp(last)
        for h in range(8):
            spread = ccol[:, h : h + 1] - crow[h : h + 1, :]
            if not fwd:
                spread = -spread
            pair = (jnp.exp(jnp.minimum(spread, 0.0)) * scores).astype(BF16)
            weighted = (turned * frow[h : h + 1, :]).astype(BF16)
            cols = pl.ds(pl.multiple_of(g * 8 * T, 8 * T) + h * T, T)
            both = nn(jnp.concatenate([pair, weighted], axis=0), rhs_ref[:, cols])
            inner_ref[:, cols] = both[:T]
            part = slice((h % 4) * T, (h % 4 + 1) * T)
            local_ref[g * 2 + h // 4, :, part] = both[T:]
            kept_ref[g * 2 + h // 4, :, part] = jnp.broadcast_to(kept[h : h + 1, :], (8, T))
        return 0

    lax.fori_loop(0, H // 8, group, 0)


def chain(
    fwd, here, exchange, proj, inner_ref, local_ref, col_ref, kept_ref,
    in_buf, out_buf, chain_sem, emit,
):
    seq = here[0]
    first, final = (0, NSEQ - 1) if fwd else (NSEQ - 1, 0)
    depth = seq if fwd else NSEQ - 1 - seq
    peer = (lax.rem(seq + (1 if fwd else NSEQ - 1), NSEQ), lax.axis_index("exp"))

    @pl.when(depth >= NSEQ // 2)
    def _():
        exchange.forward()

    @pl.when(seq == first)
    def _():
        in_buf[...] = jnp.zeros_like(in_buf)

    copies = []
    for k in range(CHUNKS):
        copy = pltpu.make_async_remote_copy(
            out_buf.at[k], in_buf.at[k], chain_sem.at[0, k], chain_sem.at[1, k],
            device_id=peer, device_id_type=MESH,
        )
        copies.append(copy)

        @pl.when(seq != first)
        def _():
            copy.wait_recv()

        state = in_buf[k]

        @pl.when(seq != final)
        def _():
            out_buf[k] = (kept_ref[k, 0:1, :] * state.astype(F32) + local_ref[k]).astype(BF16)
            copy.start()

        carried = nn(proj, state)
        gcol = col_ref[k // 2]
        for h in range(4):
            cols = slice(k * CW + h * T, k * CW + (h + 1) * T)
            j = (k % 2) * 4 + h
            emit(cols, inner_ref[:, cols] + gcol[:, j : j + 1] * carried[:, h * T : (h + 1) * T])

    @pl.when(depth < NSEQ // 2)
    def _():
        exchange.forward()

    @pl.when(seq != final)
    def _():
        for copy in copies:
            copy.wait_send()


def forward_kernel(
    len_ref, x_ref, b_ref, c_ref, ld_ref, ids_ref, cot_ref,
    resid_ref, sent_ref, got_ref, stage_ref, send_ref,
    packed, inner, local, colw, kept, in_buf, out_buf, chain_sem, put_sem, *sems,
):
    here = place()
    exchange = Exchange(here, send_ref, got_ref, stage_ref, sems, False)
    pick = pick_matrix(slot_columns(ids_ref, here))

    def gather(n, _):
        cols = pl.ds(pl.multiple_of(n * CW, CW), CW)
        packed[:, cols] = nn(pick, cot_ref[:, cols]).astype(BF16)
        return 0

    lax.fori_loop(0, D // CW, gather, 0)
    put = pltpu.make_async_copy(packed, send_ref, put_sem.at[0])
    put.start()
    entry_barrier(here, True)
    put.wait()
    exchange.start_far()
    exchange.start_near(ORDER[:9])

    c = c_ref[...]
    facts = doc_facts(len_ref, here[0])
    local_terms(True, facts, ld_ref, b_ref[...], c, x_ref, inner, local, colw, kept)

    def emit(cols, value):
        resid_ref[:, cols] = value.astype(BF16)

    chain(
        True, here, exchange, c, inner, local, colw, kept, in_buf, out_buf, chain_sem, emit
    )
    total = jnp.zeros((T, CW), F32)
    for k in range(CHUNKS):
        rows = resid_ref[:, k * CW : (k + 1) * CW].astype(F32)
        total = total + rows * rows
    scale = lax.rsqrt(jnp.sum(total, axis=1, keepdims=True) / D + EPSILON)

    def gather_mixed(n, _):
        cols = pl.ds(pl.multiple_of(n * CW, CW), CW)
        mixed = (resid_ref[:, cols].astype(F32) * scale).astype(BF16)
        sent_ref[:, cols] = nn(pick, mixed).astype(BF16)
        return 0

    lax.fori_loop(0, D // CW, gather_mixed, 0)
    exchange.wait_near(ORDER[:9])
    exchange.wait_far()
    exchange.finish()


GROUP = SLOTS // 2
HTILE = 256
FTILE = 512


def expert_kernel(
    sent_ref, cot_ref, wu_hbm, wd_hbm,
    got_ref, out_ref, recv_ref, stage_ref, stage2_ref, grad_ref,
    wu, wd, cot, rows, back, act, pre_grad, packed, load_sem, *sems,
):
    here = place()
    there = Exchange(here, sent_ref, recv_ref, stage_ref, sems[:4], False)
    home = Exchange(here, grad_ref, got_ref, stage2_ref, sems[4:], True)
    loads = [
        pltpu.make_async_copy(s, d, load_sem.at[k])
        for k, (s, d) in enumerate([(cot_ref, cot), (wd_hbm, wd), (wu_hbm, wu)])
    ]
    for load in loads:
        load.start()
    entry_barrier(here, False)
    there.start_far()
    there.start_near(ORDER[:9])
    loads[0].wait()
    loads[1].wait()

    def back_tile(n, _):
        part = pl.ds(pl.multiple_of(n * HTILE, HTILE), HTILE)
        back[:, part] = nt(cot[...], wd[part, :])
        return 0

    lax.fori_loop(0, HID // HTILE, back_tile, 0)
    loads[2].wait()
    there.forward()

    puts = []
    for g in range(2):
        group = pl.ds(g * GROUP, GROUP)
        if g == 0:
            there.wait_near(ORDER[:8])
        else:
            there.wait_near(ORDER[8:9])
            there.wait_far()
        load = pltpu.make_async_copy(recv_ref.at[group], rows.at[g], load_sem.at[3 + g])
        load.start()
        load.wait()

        def up_tile(n, _):
            part = pl.ds(pl.multiple_of(n * HTILE, HTILE), HTILE)
            pre = nn(rows[g], wu[:, part])
            sig = 1.0 / (1.0 + jnp.exp(-pre))
            act[group, part] = (pre * sig).astype(BF16)
            pre_grad[group, part] = (
                back[group, part] * sig * (1.0 + pre * (1.0 - sig))
            ).astype(BF16)
            return 0

        lax.fori_loop(0, HID // HTILE, up_tile, 0)

        def grad_tile(n, _):
            part = pl.ds(pl.multiple_of(n * FTILE, FTILE), FTILE)
            packed[group, part] = nt(pre_grad[group, :], wu[part, :]).astype(BF16)
            return 0

        lax.fori_loop(0, D // FTILE, grad_tile, 0)
        put = pltpu.make_async_copy(packed.at[group], grad_ref.at[group], load_sem.at[5 + g])
        put.start()
        put.wait()
        if g == 0:
            home.start_near(ORDER[:8])
        else:
            home.start_far()
            home.start_near(ORDER[8:9])

    def out_tile(n, _):
        part = pl.ds(pl.multiple_of(n * FTILE, FTILE), FTILE)
        packed[:, part] = nn(act[...], wd[:, part]).astype(BF16)
        return 0

    lax.fori_loop(0, D // FTILE, out_tile, 0)
    put = pltpu.make_async_copy(packed, out_ref, load_sem.at[7])
    put.start()
    home.forward()
    put.wait()
    home.wait_near(ORDER[:9])
    home.wait_far()
    home.finish()
    there.finish()


def backward_kernel(
    len_ref, grad_ref, send_ref, resid_ref, cot_ref, b_ref, c_ref, ld_ref, ids_ref, gate_ref,
    output_ref, dx_ref, got_ref, stage_ref,
    dres, got, inner, local, colw, kept, in_buf, out_buf, chain_sem, load_sem, *sems,
):
    here = place()
    exchange = Exchange(here, send_ref, got_ref, stage_ref, sems, True)
    entry_barrier(here, True)
    exchange.start_far()
    exchange.start_near(ORDER[:9])
    high, low = weight_matrices(slot_columns(ids_ref, here), gate_ref)
    total = jnp.zeros((T, CW), F32)
    for k in range(CHUNKS):
        rows = resid_ref[:, k * CW : (k + 1) * CW].astype(F32)
        total = total + rows * rows
    scale = lax.rsqrt(jnp.sum(total, axis=1, keepdims=True) / D + EPSILON)

    def combine(n, total):
        cols = pl.ds(pl.multiple_of(n * CW, CW), CW)
        dmixed = nn(high, grad_ref[:, cols]) + nn(low, grad_ref[:, cols])
        inner[:, cols] = dmixed
        return total + dmixed * (resid_ref[:, cols].astype(F32) * scale)

    total = lax.fori_loop(0, D // CW, combine, jnp.zeros((T, CW), F32))
    mean = jnp.sum(total, axis=1, keepdims=True) / D

    def finish_rows(n, _):
        cols = pl.ds(pl.multiple_of(n * CW, CW), CW)
        normed = resid_ref[:, cols].astype(F32) * scale
        dres[:, cols] = (
            cot_ref[:, cols].astype(F32) + scale * (inner[:, cols] - normed * mean)
        ).astype(BF16)
        return 0

    lax.fori_loop(0, D // CW, finish_rows, 0)
    b = b_ref[...]
    facts = doc_facts(len_ref, here[0])
    local_terms(False, facts, ld_ref, b, c_ref[...], dres, inner, local, colw, kept)

    def emit(cols, value):
        dx_ref[:, cols] = value.astype(BF16)

    chain(
        False, here, exchange, b, inner, local, colw, kept, in_buf, out_buf, chain_sem, emit
    )
    exchange.wait_near(ORDER[:9])
    exchange.wait_far()
    load = pltpu.make_async_copy(got_ref, got, load_sem.at[0])
    load.start()
    load.wait()

    def combine_out(n, _):
        cols = pl.ds(pl.multiple_of(n * CW, CW), CW)
        moe = nn(high, got[:, cols]) + nn(low, got[:, cols])
        output_ref[:, cols] = (resid_ref[:, cols].astype(F32) + moe).astype(BF16)
        return 0

    lax.fori_loop(0, D // CW, combine_out, 0)
    exchange.finish()


VM = pl.BlockSpec(memory_space=pltpu.VMEM)
SM = pl.BlockSpec(memory_space=pltpu.SMEM)
HB = pl.BlockSpec(memory_space=pltpu.HBM)
ROWS = jax.ShapeDtypeStruct((SLOTS, D), BF16)
STAGE = jax.ShapeDtypeStruct((len(FAR), 2, CAP, HALF), BF16)
TOKENS = jax.ShapeDtypeStruct((T, D), BF16)
SSD_SCRATCH = [
    pltpu.VMEM((T, D), F32),
    pltpu.VMEM((CHUNKS, T, CW), F32),
    pltpu.VMEM((H // 8, T, 8), F32),
    pltpu.VMEM((CHUNKS, 8, CW), F32),
    pltpu.VMEM((CHUNKS, T, CW), BF16),
    pltpu.VMEM((CHUNKS, T, CW), BF16),
    pltpu.SemaphoreType.DMA((2, CHUNKS)),
]


def call(kernel, ident, ins, outs, out_specs, scratch):
    return pl.pallas_call(
        kernel,
        out_shape=outs,
        in_specs=ins,
        out_specs=out_specs,
        scratch_shapes=scratch,
        compiler_params=pltpu.CompilerParams(
            collective_id=ident, has_side_effects=True, vmem_limit_bytes=VMEM_LIMIT
        ),
    )


def on_device(
    inputs, b_proj, c_proj, log_decay, doc_lengths, expert_ids, gate_weights, w_up, w_down,
    cotangent,
):
    x, b, c, ld, ids = (inputs[0], b_proj[0], c_proj[0], log_decay[0], expert_ids[0])
    resid, sent, got_cot, _, _ = call(
        forward_kernel, 1,
        [SM] + [VM] * 6,
        [TOKENS, ROWS, ROWS, STAGE, ROWS],
        [VM, VM, HB, HB, HB],
        [pltpu.VMEM((SLOTS, D), BF16)]
        + SSD_SCRATCH
        + [pltpu.SemaphoreType.DMA((1,))]
        + EXCHANGE_SEMS,
    )(doc_lengths, x, b, c, ld, ids, cotangent[0])
    got_grad, out_rows, _, _, _, _ = call(
        expert_kernel, 2,
        [HB] * 4,
        [ROWS, ROWS, ROWS, STAGE, STAGE, ROWS],
        [HB] * 6,
        [
            pltpu.VMEM((D, HID), BF16),
            pltpu.VMEM((HID, D), BF16),
            pltpu.VMEM((SLOTS, D), BF16),
            pltpu.VMEM((2, GROUP, D), BF16),
            pltpu.VMEM((SLOTS, HID), F32),
            pltpu.VMEM((SLOTS, HID), BF16),
            pltpu.VMEM((SLOTS, HID), BF16),
            pltpu.VMEM((SLOTS, D), BF16),
            pltpu.SemaphoreType.DMA((8,)),
        ]
        + EXCHANGE_SEMS * 2,
    )(sent, got_cot, w_up[0], w_down[0])
    output, dx, _, _ = call(
        backward_kernel, 3,
        [SM, VM, HB] + [VM] * 7,
        [TOKENS, TOKENS, ROWS, STAGE],
        [VM, VM, HB, HB],
        [pltpu.VMEM((T, D), BF16), pltpu.VMEM((SLOTS, D), BF16)]
        + SSD_SCRATCH
        + [pltpu.SemaphoreType.DMA((1,))]
        + EXCHANGE_SEMS,
    )(
        doc_lengths, got_grad, out_rows, resid, cotangent[0], b, c, ld, ids, gate_weights[0]
    )
    return (output[None], dx[None])


def solution(mesh):
    rows = P("exp", "seq", None)
    whole = P("exp", None, None)
    return jax.shard_map(
        on_device,
        mesh=mesh,
        in_specs=(
            rows, rows, rows, P("exp", None, "seq"), P("exp", None), rows, rows, whole, whole,
            rows,
        ),
        out_specs=(rows, rows),
        check_vma=False,
    )
```

time: 433 us -> 194 us (0.45)
  the two profiles are of different devices: /device:TPU:1 before, /device:TPU:50 now
where the time goes in v1:
time: 194 us; the launch traced here: 193 us
  Pallas kernels  186 us (96%)
  local copies, waits for them, and re-layouts  6.74 us (3%)
    pallas_call x1, Pallas kernels, on_device(): call(expert_kernel, 2, [HB] * 4, [ROWS, ROWS, ROWS, STAGE, STAGE, ROWS],...  81.3 us
    pallas_call x1, Pallas kernels, on_device(): call(backward_kernel, 3, [SM, VM, HB] + [VM] * 7, [TOKENS, TOKENS, ROWS,...  53.6 us
    pallas_call x1, Pallas kernels, on_device(): call(forward_kernel, 1, [SM] + [VM] * 6, [TOKENS, ROWS, ROWS, STAGE, ROWS...  51 us
    unnamed x6, local copies, waits for them, and re-layouts  6.74 us

profile of v1, /device:TPU:50, one launch (start us, length us, event | category | flops | bytes accessed | tf_op | source)
XLA Modules:
  0.0 193.3 jit_solution(10582255523831317000)
XLA Ops:
  0.6 1.4 copy.12
  2.0 51.0 %shard_map.113 = (bf16[128,4096]{1,0:T(8,128)(2,1)}, bf16[384,4096]{1,0:T(8,128)(2,1)}, bf16[384,4096]{1,0:T(8,128)(2,1)}, bf16[7,2,24,2048]{3,2,1,0:T(8,128)(2,1)}, bf16[384,4096]{1,0:T(8,128)(2,1)}) custom-call(s32[1,6]{1,0:T(1,128)} %len_ref.3, bf16[128,4096]{1,0:T(8,128)(2,1)} %bitcast.15, bf16[128,128]{1,0:T(8,128)(2,1)} %bitcast.21, ...), custom_call_target="tpu_custom_call" | custom-call | tf_op jit(solution)/shard_map/pallas_call | solution.py:557
  53.0 0.0 copy-start
  53.1 81.3 %shard_map.114 = (bf16[384,4096]{1,0:T(8,128)(2,1)}, bf16[384,4096]{1,0:T(8,128)(2,1)}, bf16[384,4096]{1,0:T(8,128)(2,1)}, bf16[7,2,24,2048]{3,2,1,0:T(8,128)(2,...) custom-call(bf16[384,4096]{1,0:T(8,128)(2,1)} %get-tuple-element.9.sent_ref, ...), custom_call_target="tpu_custom_call" | custom-call | tf_op jit(solution)/shard_map/pallas_call | solution.py:567
  134.4 0.0 copy-done
  134.4 0.7 copy.13
  135.1 53.6 %shard_map.115 = (bf16[128,4096]{1,0:T(8,128)(2,1)}, bf16[128,4096]{1,0:T(8,128)(2,1)}, bf16[384,4096]{1,0:T(8,128)(2,1)}, bf16[7,2,24,2048]{3,2,1,0:T(8,128)(2,1)}) custom-call(s32[1,6]{1,0:T(1,128)} %len_ref.3, bf16[384,4096]{1,0:T(8,128)(2,1)} %get-tuple-element.11.grad_ref, bf16[384,4096]{1,0:T(8,128)(2,1)} %get-tuple-element.12.send_ref, ...), custom_call_target="tpu_custom_call" | custom-call | tf_op jit(solution)/shard_map/pallas_call | solution.py:585
  188.8 2.3 %copy.16 = bf16[1,128,4096]{2,1,0:T(8,128)(2,1)} copy(bf16[1,128,4096]{2,1,0:T(8,128)(2,1)} %bitcast.17) | data formatting | bytes 2097152
  191.0 2.3 %copy.17 = bf16[1,128,4096]{2,1,0:T(8,128)(2,1)} copy(bf16[1,128,4096]{2,1,0:T(8,128)(2,1)} %bitcast.16) | data formatting | bytes 2097152
Async XLA Ops:
  53.0 81.3 %copy-start = (f32[1,128,2]{1,2,0:T(2,128)S(1)}, f32[1,128,2]{1,2,0:T(2,128)}, u32[]{:S(2)}) copy-start(f32[1,128,2]{1,2,0:T(2,128)} %param.16) | copy-start | bytes 3076

commit v2 on v1

v2 whole, which is shorter than its diff:
```python
import functools
import jax
import jax.numpy as jnp
from jax import lax
from jax.experimental import pallas as pl
from jax.experimental.pallas import tpu as pltpu
from jax.sharding import PartitionSpec as P

MESH = pl.DeviceIdType.MESH
F32, BF16, I32 = jnp.float32, jnp.bfloat16, jnp.int32
HIGHEST = lax.Precision.HIGHEST
EPSILON = 1e-06

T = 128
D = 4096
HID = 1024
H = 32
CAP = 24
SLOTS = 16 * CAP
NSEQ = 8
CHUNKS = 8
CW = D // CHUNKS
HALF = D // 2
VMEM_LIMIT = 62 * 1024 * 1024

NEAR = [(0, 1), (1, 0), (0, 3), (3, 0), (1, 1), (3, 3), (1, 3), (3, 1)]
FAR = [(dx, dy) for dx in range(4) for dy in range(4) if 2 in (dx, dy)]
ORDER = [(0, 0)] + NEAR + FAR


def code_row(d):
    return (d[1] * 4 + d[0]) * CAP


def slot_row(d):
    return ORDER.index(d) * CAP


def flip(d):
    return ((4 - d[0]) % 4, (4 - d[1]) % 4)


def place():
    me = lax.axis_index("exp")
    return lax.axis_index("seq"), lax.rem(me, 4), me // 4


def at(here, d):
    seq, x, y = here
    return (seq, lax.rem(y + d[1], 4) * 4 + lax.rem(x + d[0], 4))


def greet(here):
    barrier = pltpu.get_barrier_semaphore()
    for d in NEAR:
        pl.semaphore_signal(barrier, inc=1, device_id=at(here, d), device_id_type=MESH)
    for k in (1, NSEQ - 1):
        peer = (lax.rem(here[0] + k, NSEQ), lax.axis_index("exp"))
        pl.semaphore_signal(barrier, inc=1, device_id=peer, device_id_type=MESH)


def wait_for_all():
    pl.semaphore_wait(pltpu.get_barrier_semaphore(), len(NEAR) + 2)


EXCHANGE_SEMS = [
    pltpu.SemaphoreType.DMA((2, len(NEAR))),
    pltpu.SemaphoreType.DMA((2, len(FAR), 2)),
    pltpu.SemaphoreType.DMA((2, len(FAR), 2)),
    pltpu.SemaphoreType.DMA((1,)),
]


class Exchange:
    def __init__(self, here, src, dst, stage, sems, back):
        near_sem, far_sem, fwd_sem, self_sem = sems
        src_row, dst_row = (slot_row, code_row) if back else (code_row, slot_row)

        def rows(ref, start):
            return ref.at[pl.ds(start, CAP)]

        self.own = pltpu.make_async_copy(
            rows(src, src_row((0, 0))), rows(dst, dst_row((0, 0))), self_sem.at[0]
        )
        self.near = {}
        for k, d in enumerate(NEAR):
            self.near[d] = pltpu.make_async_remote_copy(
                rows(src, src_row(d)),
                rows(dst, dst_row(d)),
                near_sem.at[0, k],
                near_sem.at[1, k],
                device_id=at(here, flip(d) if back else d),
                device_id_type=MESH,
            )
        self.far, self.fwd = ([], [])
        for j, d in enumerate(FAR):
            v = flip(d) if back else d
            for q, sign in enumerate((1, 3) if j % 2 else (3, 1)):
                leg = tuple(sign if a == 2 else a for a in v)
                rest = tuple((a - b) % 4 for a, b in zip(v, leg))
                cols = pl.ds(q * HALF, HALF)
                self.far.append(
                    pltpu.make_async_remote_copy(
                        src.at[pl.ds(src_row(d), CAP), cols],
                        stage.at[j, q],
                        far_sem.at[0, j, q],
                        far_sem.at[1, j, q],
                        device_id=at(here, leg),
                        device_id_type=MESH,
                    )
                )
                self.fwd.append(
                    pltpu.make_async_remote_copy(
                        stage.at[j, q],
                        dst.at[pl.ds(dst_row(d), CAP), cols],
                        fwd_sem.at[0, j, q],
                        fwd_sem.at[1, j, q],
                        device_id=at(here, rest),
                        device_id_type=MESH,
                    )
                )

    def start_far(self, half):
        for c in self.far[half::2]:
            c.start()

    def start_near(self, which):
        for d in which:
            if d == (0, 0):
                self.own.start()
            else:
                self.near[d].start()

    def forward(self):
        for c, f in zip(self.far, self.fwd):
            c.wait_recv()
            f.start()

    def wait_near(self, which):
        for d in which:
            if d == (0, 0):
                self.own.wait()
            else:
                self.near[d].wait_recv()

    def wait_far(self):
        for f in self.fwd:
            f.wait_recv()

    def finish(self):
        for c in list(self.near.values()) + self.far + self.fwd:
            c.wait_send()


def iota(shape, dim):
    return lax.broadcasted_iota(I32, shape, dim)


def nt(a, b, precision=None):
    return lax.dot_general(
        a, b, (((1,), (1,)), ((), ())), precision=precision, preferred_element_type=F32
    )


def nn(a, b, precision=None):
    return jnp.dot(a, b, precision=precision, preferred_element_type=F32)


def to_column(row):
    eye = iota((T, T), 0) == iota((T, T), 1)
    return jnp.sum(jnp.where(eye, row, 0.0), axis=1, keepdims=True)


def slot_columns(ids_ref, here):
    seq, x, y = here
    codes = []
    for j in range(2):
        e = ids_ref[j : j + 1, :]
        code = (((e // 4) - y) & 3) * 4 + (((e & 3) - x) & 3)
        codes.append(to_column(code.astype(F32)).astype(I32))
    lane = iota((T, T), 1)
    named = [lane == code for code in codes]
    both = jnp.where(named[0] | named[1], 1.0, 0.0).astype(BF16)
    earlier = jnp.where(iota((T, T), 1) < iota((T, T), 0), 1.0, 0.0).astype(BF16)
    rank = nn(earlier, both)
    return [
        code * CAP + jnp.sum(jnp.where(n, rank, 0.0), axis=1, keepdims=True).astype(I32)
        for code, n in zip(codes, named)
    ]


def pick_matrix(slots):
    eye = iota((T, T), 0) == iota((T, T), 1)
    s = iota((SLOTS, T), 0)
    hit = None
    for slot in slots:
        row = jnp.sum(jnp.where(eye, slot, 0), axis=0, keepdims=True)
        hit = (s == row) if hit is None else hit | (s == row)
    return jnp.where(hit, 1.0, 0.0).astype(BF16)


def weight_matrices(slots, gate_ref):
    s = iota((T, SLOTS), 1)
    w = jnp.zeros((T, SLOTS), F32)
    for j, slot in enumerate(slots):
        w = w + jnp.where(s == slot, to_column(gate_ref[j : j + 1, :]), 0.0)
    high = w.astype(BF16)
    return high, (w - high.astype(F32)).astype(BF16)


def doc_facts(len_ref, seq):
    base = seq * T
    starts = [jnp.int32(0)]
    for j in range(5):
        starts.append(starts[-1] + len_ref[0, j])

    def doc(pos):
        total = jnp.where(starts[0] <= pos, 1, 0)
        for s in starts[1:]:
            total = total + jnp.where(s <= pos, 1, 0)
        return total - 1

    row, col = doc(base + iota((1, T), 1)), doc(base + iota((T, 1), 0))
    return row, col, doc(base - 1), doc(base + T - 1)


class Pass:
    def __init__(self, fwd, here, facts, ld_ref, b, c, rhs_ref, refs, in_buf, out_buf, sem):
        self.fwd, self.seq, self.ld_ref, self.rhs_ref = (fwd, here[0], ld_ref, rhs_ref)
        self.lhs, self.inner, self.local, self.colw, self.kept = refs
        self.in_buf, self.out_buf, self.sem = (in_buf, out_buf, sem)
        self.proj = c if fwd else b
        doc_row, doc_col, before, last_doc = facts
        down, across = iota((T, T), 0), iota((T, T), 1)
        other = b if fwd else c
        causal = (down >= across) if fwd else (across >= down)
        self.scores = jnp.where(causal & (doc_col == doc_row), nt(self.proj, other), 0.0)
        eye = jnp.where(down == across, 1.0, 0.0).astype(BF16)
        self.turned = nt(eye, other)
        self.upto = jnp.where(down <= across, 1.0, 0.0)
        self.upto_t = jnp.where(across <= down, 1.0, 0.0)
        self.opened_e = jnp.where(last_doc == before, 1.0, 0.0)
        row_doc, col_doc = (last_doc, before) if fwd else (before, last_doc)
        self.row_mask = jnp.where(doc_row == row_doc, 1.0, 0.0)
        self.col_mask = jnp.where(doc_col == col_doc, 1.0, 0.0)

    def prepare(self, g):
        ld = self.ld_ref[pl.ds(pl.multiple_of(g * 8, 8), 8), :]
        crow = nn(ld, self.upto, HIGHEST)
        ccol = nt(self.upto_t, ld, HIGHEST)
        last = crow[:, T - 1 : T]
        if self.fwd:
            frow = self.row_mask * jnp.exp(last - crow)
            self.colw[g] = self.col_mask * jnp.exp(ccol)
        else:
            frow = self.row_mask * jnp.exp(crow)
            self.colw[g] = self.col_mask * jnp.exp(ccol[T - 1 : T, :] - ccol)
        kept = self.opened_e * jnp.exp(last)
        for h in range(8):
            spread = ccol[:, h : h + 1] - crow[h : h + 1, :]
            if not self.fwd:
                spread = -spread
            pair = jnp.exp(jnp.minimum(spread, 0.0)) * self.scores
            self.lhs[g * 8 + h, :T, :] = pair.astype(BF16)
            self.lhs[g * 8 + h, T:, :] = (self.turned * frow[h : h + 1, :]).astype(BF16)
            part = slice((h % 4) * T, (h % 4 + 1) * T)
            self.kept[g * 2 + h // 4, :, part] = jnp.broadcast_to(kept[h : h + 1, :], (8, T))

    def apply(self, g):
        for h in range(8):
            cols = pl.ds(pl.multiple_of(g * 8 * T, 8 * T) + h * T, T)
            both = nn(self.lhs[g * 8 + h], self.rhs_ref[:, cols])
            self.inner[:, cols] = both[:T]
            part = slice((h % 4) * T, (h % 4 + 1) * T)
            self.local[g * 2 + h // 4, :, part] = both[T:]

    def run(self, group, forward, turns, emit):
        first, final = (0, NSEQ - 1) if self.fwd else (NSEQ - 1, 0)
        seq = self.seq
        depth = seq if self.fwd else NSEQ - 1 - seq
        step = 1 if self.fwd else NSEQ - 1
        peer = (lax.rem(seq + step, NSEQ), lax.axis_index("exp"))

        @pl.when(seq == first)
        def _():
            self.in_buf[...] = jnp.zeros_like(self.in_buf)

        @pl.when(seq != first)
        def _():
            def each(g, _):
                group(g)
                return 0

            lax.fori_loop(0, H // 8, each, 0)

        copies = []
        for k in range(CHUNKS + 1):
            depths = [d for d in range(NSEQ) if turns[d] == k]
            if depths:

                @pl.when((depth >= depths[0]) & (depth <= depths[-1]))
                def _():
                    forward()

            if k == CHUNKS:
                break
            if k % 2 == 0:

                @pl.when(seq == first)
                def _():
                    group(k // 2)

            copy = pltpu.make_async_remote_copy(
                self.out_buf.at[k], self.in_buf.at[k], self.sem.at[0, k], self.sem.at[1, k],
                device_id=peer, device_id_type=MESH,
            )
            copies.append(copy)

            @pl.when(seq != first)
            def _():
                copy.wait_recv()

            state = self.in_buf[k]

            @pl.when(seq != final)
            def _():
                handed = self.kept[k, 0:1, :] * state.astype(F32) + self.local[k]
                self.out_buf[k] = handed.astype(BF16)
                copy.start()

            carried = nn(self.proj, state)
            colw = self.colw[k // 2]
            for h in range(4):
                cols = slice(k * CW + h * T, k * CW + (h + 1) * T)
                j = (k % 2) * 4 + h
                state_term = colw[:, j : j + 1] * carried[:, h * T : (h + 1) * T]
                emit(cols, self.inner[:, cols] + state_term)

        @pl.when(seq != final)
        def _():
            for copy in copies:
                copy.wait_send()


GROUP = SLOTS // 2
HTILE = 256
FTILE = 512


def columns(n, width):
    return pl.ds(pl.multiple_of(n * width, width), width)


def gather_half(half, pick, packed, send_ref, put_sem, tile):
    def step(n, _):
        cols = columns(n, CW)
        packed[:, cols] = nn(pick, tile(cols)).astype(BF16)
        return 0

    lax.fori_loop(half * (HALF // CW), (half + 1) * (HALF // CW), step, 0)
    cols = pl.ds(half * HALF, HALF)
    put = pltpu.make_async_copy(packed.at[:, cols], send_ref.at[:, cols], put_sem)
    put.start()
    return put


def row_scale(resid):
    total = jnp.zeros((T, CW), F32)
    for k in range(CHUNKS):
        rows = resid[:, k * CW : (k + 1) * CW].astype(F32)
        total = total + rows * rows
    return lax.rsqrt(jnp.sum(total, axis=1, keepdims=True) / D + EPSILON)


def layer_kernel(
    len_ref, x_hbm, b_hbm, c_hbm, ld_hbm, ids_ref, gate_ref, wu_hbm, wd_hbm, cot_hbm,
    resid_hbm, dx_hbm, high_hbm, low_hbm, got4,
    send1, got1, stage1, send2, got2, stage2, send3, got3, stage3, send4, stage4,
    x_ref, cot_ref, b_ref, c_ref, ld_ref, resid, dres, dx_ref, high_ref, low_ref,
    packed, got, rows, wu, wd, back, act, pre_grad,
    lhs, inner, local, colw, kept, fwd_in, bwd_in, out_buf, chain_sem, load_sem, put_sem, *sems,
):
    here = place()
    first = Exchange(here, send1, got1, stage1, sems[0:4], False)
    second = Exchange(here, send2, got2, stage2, sems[4:8], False)
    third = Exchange(here, send3, got3, stage3, sems[8:12], True)
    fourth = Exchange(here, send4, got4, stage4, sems[12:16], True)

    def load(k, src, dst):
        copy = pltpu.make_async_copy(src, dst, load_sem.at[k])
        copy.start()
        return copy

    cot_load = load(0, cot_hbm, cot_ref)
    loads = [
        load(1 + k, s, d)
        for k, (s, d) in enumerate(
            [(x_hbm, x_ref), (b_hbm, b_ref), (c_hbm, c_ref), (ld_hbm, ld_ref)]
        )
    ]
    greet(here)
    slots = slot_columns(ids_ref, here)
    pick = pick_matrix(slots)
    cot_load.wait()

    puts = [
        gather_half(h, pick, packed, send1, put_sem.at[h], lambda cols: cot_ref[:, cols])
        for h in range(2)
    ]
    puts[0].wait()
    wait_for_all()
    first.start_far(0)
    puts[1].wait()
    first.start_far(1)
    first.start_near(ORDER[:9])
    wd_load = load(5, wd_hbm, wd)
    wu_load = load(6, wu_hbm, wu)
    for copy in loads:
        copy.wait()
    b, c = b_ref[...], c_ref[...]
    facts = doc_facts(len_ref, here[0])
    refs = (lhs, inner, local, colw, kept)
    ahead = Pass(
        True, here, facts, ld_ref, b, c, x_ref, refs, fwd_in, out_buf.at[0], chain_sem.at[0]
    )

    def both(g):
        ahead.prepare(g)
        ahead.apply(g)

    def emit_resid(cols, value):
        resid[:, cols] = value.astype(BF16)

    ahead.run(both, first.forward, (8, 6, 5, 3, 0, 0, 0, 0), emit_resid)
    resid_put = pltpu.make_async_copy(resid, resid_hbm, put_sem.at[8])
    resid_put.start()
    scale = row_scale(resid)

    puts = [
        gather_half(
            h, pick, packed, send2, put_sem.at[2 + h],
            lambda cols: (resid[:, cols].astype(F32) * scale).astype(BF16),
        )
        for h in range(2)
    ]
    puts[0].wait()
    second.start_far(0)
    puts[1].wait()
    second.start_far(1)
    second.start_near(ORDER[:9])

    first.wait_near(ORDER[:9])
    first.wait_far()
    load(7, got1, got).wait()
    wd_load.wait()

    def back_tile(n, _):
        part = columns(n, HTILE)
        back[:, part] = nt(got[...], wd[part, :])
        return 0

    lax.fori_loop(0, HID // HTILE, back_tile, 0)
    wu_load.wait()
    second.forward()
    for g in range(2):
        group = pl.ds(g * GROUP, GROUP)
        if g == 0:
            second.wait_near(ORDER[:8])
        else:
            second.wait_near(ORDER[8:9])
            second.wait_far()
        load(8 + g, got2.at[group], rows.at[g]).wait()

        def up_tile(n, _):
            part = columns(n, HTILE)
            pre = nn(rows[g], wu[:, part])
            sig = 1.0 / (1.0 + jnp.exp(-pre))
            act[group, part] = (pre * sig).astype(BF16)
            pre_grad[group, part] = (
                back[group, part] * sig * (1.0 + pre * (1.0 - sig))
            ).astype(BF16)
            return 0

        lax.fori_loop(0, HID // HTILE, up_tile, 0)

        def grad_tile(n, _):
            part = columns(n, FTILE)
            packed[group, part] = nt(pre_grad[group, :], wu[part, :]).astype(BF16)
            return 0

        lax.fori_loop(0, D // FTILE, grad_tile, 0)
        put = pltpu.make_async_copy(packed.at[group], send3.at[group], put_sem.at[4 + g])
        put.start()
        put.wait()
        if g == 0:
            third.start_near(ORDER[:8])
        else:
            third.start_far(0)
            third.start_far(1)
            third.start_near(ORDER[8:9])

    def out_tile(n, _):
        part = columns(n, FTILE)
        packed[:, part] = nn(act[...], wd[:, part]).astype(BF16)
        return 0

    lax.fori_loop(0, D // FTILE, out_tile, 0)
    out_put = pltpu.make_async_copy(packed, send4, put_sem.at[6])
    out_put.start()
    high, low = weight_matrices(slots, gate_ref)
    high_ref[...] = high
    low_ref[...] = low
    weight_puts = [
        pltpu.make_async_copy(s, d, put_sem.at[9 + k])
        for k, (s, d) in enumerate([(high_ref, high_hbm), (low_ref, low_hbm)])
    ]
    for put in weight_puts:
        put.start()
    third.forward()
    out_put.wait()

    fourth.start_far(0)
    fourth.start_far(1)
    fourth.start_near(ORDER[:9])
    behind = Pass(
        False, here, facts, ld_ref, b, c, dres, refs, bwd_in, out_buf.at[1], chain_sem.at[1]
    )

    def prepare(g, _):
        behind.prepare(g)
        return 0

    lax.fori_loop(0, H // 8, prepare, 0)
    third.wait_near(ORDER[:9])
    third.wait_far()
    load(10, got3, got).wait()

    def combine(n, total):
        cols = columns(n, CW)
        dmixed = nn(high, got[:, cols]) + nn(low, got[:, cols])
        inner[:, cols] = dmixed
        return total + dmixed * (resid[:, cols].astype(F32) * scale)

    total = lax.fori_loop(0, D // CW, combine, jnp.zeros((T, CW), F32))
    mean = jnp.sum(total, axis=1, keepdims=True) / D

    def finish_rows(n, _):
        cols = columns(n, CW)
        normed = resid[:, cols].astype(F32) * scale
        dres[:, cols] = (
            cot_ref[:, cols].astype(F32) + scale * (inner[:, cols] - normed * mean)
        ).astype(BF16)
        return 0

    lax.fori_loop(0, D // CW, finish_rows, 0)

    def emit_dx(cols, value):
        dx_ref[:, cols] = value.astype(BF16)

    behind.run(behind.apply, fourth.forward, (0,) * NSEQ, emit_dx)
    dx_put = pltpu.make_async_copy(dx_ref, dx_hbm, put_sem.at[7])
    dx_put.start()
    fourth.wait_near(ORDER[:9])
    fourth.wait_far()
    dx_put.wait()
    resid_put.wait()
    for put in weight_puts:
        put.wait()
    for exchange in (first, second, third, fourth):
        exchange.finish()


def output_kernel(high_ref, low_ref, got_ref, resid_ref, dx_ref, output_ref, grad_ref):
    def step(n, _):
        cols = columns(n, CW)
        moe = nn(high_ref[...], got_ref[:, cols]) + nn(low_ref[...], got_ref[:, cols])
        output_ref[:, cols] = (resid_ref[:, cols].astype(F32) + moe).astype(BF16)
        grad_ref[:, cols] = dx_ref[:, cols]
        return 0

    lax.fori_loop(0, D // CW, step, 0)


VM = pl.BlockSpec(memory_space=pltpu.VMEM)
SM = pl.BlockSpec(memory_space=pltpu.SMEM)
HB = pl.BlockSpec(memory_space=pltpu.HBM)
ROWS = jax.ShapeDtypeStruct((SLOTS, D), BF16)
STAGE = jax.ShapeDtypeStruct((len(FAR), 2, CAP, HALF), BF16)
TOKENS = jax.ShapeDtypeStruct((T, D), BF16)
WEIGHTS = jax.ShapeDtypeStruct((T, SLOTS), BF16)


def on_device(
    inputs, b_proj, c_proj, log_decay, doc_lengths, expert_ids, gate_weights, w_up, w_down,
    cotangent,
):
    outs = [TOKENS, TOKENS, WEIGHTS, WEIGHTS, ROWS]
    outs += [ROWS, ROWS, STAGE] * 3 + [ROWS, STAGE]
    resid, dx, high, low, got = pl.pallas_call(
        layer_kernel,
        out_shape=outs,
        in_specs=[SM] + [HB] * 4 + [VM] * 2 + [HB] * 3,
        out_specs=[HB] * len(outs),
        scratch_shapes=[
            pltpu.VMEM((T, D), BF16),
            pltpu.VMEM((T, D), BF16),
            pltpu.VMEM((T, T), BF16),
            pltpu.VMEM((T, T), BF16),
            pltpu.VMEM((H, T), F32),
            pltpu.VMEM((T, D), BF16),
            pltpu.VMEM((T, D), BF16),
            pltpu.VMEM((T, D), BF16),
            pltpu.VMEM((T, SLOTS), BF16),
            pltpu.VMEM((T, SLOTS), BF16),
            pltpu.VMEM((SLOTS, D), BF16),
            pltpu.VMEM((SLOTS, D), BF16),
            pltpu.VMEM((2, GROUP, D), BF16),
            pltpu.VMEM((D, HID), BF16),
            pltpu.VMEM((HID, D), BF16),
            pltpu.VMEM((SLOTS, HID), F32),
            pltpu.VMEM((SLOTS, HID), BF16),
            pltpu.VMEM((SLOTS, HID), BF16),
            pltpu.VMEM((H, 2 * T, T), BF16),
            pltpu.VMEM((T, D), F32),
            pltpu.VMEM((CHUNKS, T, CW), F32),
            pltpu.VMEM((H // 8, T, 8), F32),
            pltpu.VMEM((CHUNKS, 8, CW), F32),
            pltpu.VMEM((CHUNKS, T, CW), BF16),
            pltpu.VMEM((CHUNKS, T, CW), BF16),
            pltpu.VMEM((2, CHUNKS, T, CW), BF16),
            pltpu.SemaphoreType.DMA((2, 2, CHUNKS)),
            pltpu.SemaphoreType.DMA((11,)),
            pltpu.SemaphoreType.DMA((11,)),
        ]
        + EXCHANGE_SEMS * 4,
        compiler_params=pltpu.CompilerParams(
            collective_id=1, has_side_effects=True, vmem_limit_bytes=VMEM_LIMIT
        ),
    )(
        doc_lengths, inputs[0], b_proj[0], c_proj[0], log_decay[0], expert_ids[0].T,
        gate_weights[0].T, w_up[0], w_down[0], cotangent[0],
    )[:5]
    output, grad = pl.pallas_call(
        output_kernel,
        out_shape=[TOKENS, TOKENS],
        in_specs=[VM] * 5,
        out_specs=[VM, VM],
        compiler_params=pltpu.CompilerParams(vmem_limit_bytes=VMEM_LIMIT),
    )(high, low, got, resid, dx)
    return (output[None], grad[None])


def solution(mesh):
    rows = P("exp", "seq", None)
    whole = P("exp", None, None)
    return jax.shard_map(
        on_device,
        mesh=mesh,
        in_specs=(
            rows, rows, rows, P("exp", None, "seq"), P("exp", None), rows, rows, whole, whole,
            rows,
        ),
        out_specs=(rows, rows),
        check_vma=False,
    )
```

time: 194 us -> 180 us (0.928)
  the two profiles are of different devices: /device:TPU:50 before, /device:TPU:1 now
where the time goes in v2:
time: 180 us
  Pallas kernels  179 us (99%)
    pallas_call x1, Pallas kernels, on_device(): pl.pallas_call(layer_kernel, out_shape=outs, in_specs=[SM] + [HB] * 4 + [...  173 us
    pallas_call x1, Pallas kernels, on_device(): pl.pallas_call(output_kernel, out_shape=[TOKENS, TOKENS], in_specs=[VM] *...  6.25 us

profile of v2, /device:TPU:1, one launch (start us, length us, event | category | flops | bytes accessed | tf_op | source)
XLA Modules:
  0.0 180.0 jit_solution(6724012897413884130)
XLA Ops:
  0.6 173.1 %shard_map.113 = (bf16[128,4096]{1,0:T(8,128)(2,1)}, bf16[128,4096]{1,0:T(8,128)(2,1)}, bf16[128,384]{1,0:T(8,128)(2,1)}, bf16[128,384]{1,0:T(8,128)(2,1)}, bf16...) custom-call(s32[1,6]{1,0:T(1,128)} %len_ref.1, ...), custom_call_target="tpu_custom_call" | custom-call | tf_op jit(solution)/shard_map/pallas_call | solution.py:599
  173.7 6.3 %shard_map.114 = (bf16[128,4096]{1,0:T(8,128)(2,1)}, bf16[128,4096]{1,0:T(8,128)(2,1)}) custom-call(bf16[128,384]{1,0:T(8,128)(2,1)} %get-tuple-element.9.high_ref, bf16[128,384]{1,0:T(8,128)(2,1)} %get-tuple-element.10.low_ref, bf16[384,4096]{1,0:T(8,128)(2,1)} %get-tuple-element.11.got_ref, bf16[128,4096]{1,0:T(8,128)(2,1)} %get-tuple-element.12.resid_ref, ...), custom_call_target="tpu_custom_call" | custom-call | tf_op jit(solution)/shard_map/pallas_call | solution.py:643
